TPU v7x, 32 devices: a whole 2x2x4 slice. The times are simulated.
32 devices in a mesh: depth: 8 (over y, x, core), lane: 4 (over z).
Axes of the slice: x: 2, y: 2, z: 4, core: 2. Of those that a mesh axis runs over, the one named last changes fastest.
Arguments:
- fields_in: float32 [8, 4, 16, 1024], P('depth', None, 'lane'), may hold values from -6 to 6
- shot_data: float32 [4, 16, 2, 16, 1024], P(None, 'depth', None, 'lane'), may hold values from -1.5 to 1.5
- codes: int32 [4, 16, 16], P(None, None, 'lane'), may hold values from 0 to 15
- vel_index: int32 [32, 1024], P('depth'), may hold values from 0 to 63
- slowness_table: float32 [64], replicated, may hold values from 0.4 to 1
Outputs:
- fields_out: float32 [8, 4, 16, 1024], P('depth', None, 'lane')
- image: float32 [32, 1024], P(('depth', 'lane'))
All inputs are finite; a program needn't handle non-finite values.
Results may differ from a plain program's by a relative error of at most 0.0003.
Values sent between devices are 32-bit elements; how exact they have to be, the bound alone decides.
A program may use at most 64 MiB of HBM per device.

v0:
```python
import functools
import math

import jax
import jax.numpy as jnp
import numpy as np
from jax import lax
from jax.experimental import pallas as pl
from jax.experimental.pallas import tpu as pltpu
from jax.sharding import PartitionSpec as P

MESH = pl.DeviceIdType.MESH
CODES = 16
OMEGA_LO = 0.25
OMEGA_STEP = 0.07
DEPTH_STEP = 1.0
TWO_PI = 6.283185307179586
LANES = 128
BF16 = jnp.bfloat16
F32 = jnp.float32


def dft_matrix(count):
    turns = np.outer(np.arange(count), np.arange(count)) % count
    angle = turns * (2.0 * np.pi / count)
    c, s = np.cos(angle), np.sin(angle)
    full = np.block([[c, -s], [s, c]]).astype(np.float32)
    high = full.astype(BF16)
    low = (full - high.astype(np.float32)).astype(BF16)
    return high, low


def twist_tables(outer, inner):
    angle = np.outer(np.arange(outer), np.arange(inner)) * (2.0 * np.pi / (outer * inner))
    return np.stack([np.cos(angle), np.sin(angle)]).astype(np.float32)


def sincos(x):
    n = jnp.floor(x * (2.0 / math.pi) + 0.5)
    r = x - n * 1.5703125
    r = r - n * 4.837512969970703e-4
    r = r - n * 7.549789948768648e-8
    z = r * r
    s = r + r * z * (-1.6666654611e-1 + z * (8.3321608736e-3 + z * -1.9515295891e-4))
    c = 1.0 - 0.5 * z + z * z * (
        4.166664568298827e-2 + z * (-1.388731625493765e-3 + z * 2.443315711809948e-5)
    )
    q = n - 4.0 * jnp.floor(n * 0.25)
    odd = (q == 1.0) | (q == 3.0)
    sin_base = jnp.where(odd, c, s)
    cos_base = jnp.where(odd, s, c)
    sin_out = jnp.where(q >= 2.0, -sin_base, sin_base)
    cos_out = jnp.where((q == 1.0) | (q == 2.0), -cos_base, cos_base)
    return sin_out, cos_out


def dft_across(re, im):
    count = len(re)
    if count == 1:
        return re, im
    even_re, even_im = dft_across(re[0::2], im[0::2])
    odd_re, odd_im = dft_across(re[1::2], im[1::2])
    half = count // 2
    out_re, out_im = [None] * count, [None] * count
    for k in range(half):
        c = math.cos(2.0 * math.pi * k / count)
        s = math.sin(2.0 * math.pi * k / count)
        a, b = odd_re[k], odd_im[k]
        if k == 0:
            tr, ti = a, b
        elif 4 * k == count:
            tr, ti = b, -a
        elif 8 * k == count:
            tr, ti = (a + b) * c, (b - a) * c
        elif 8 * k == 3 * count:
            tr, ti = (b - a) * s, -(a + b) * s
        else:
            tr, ti = a * c + b * s, b * c - a * s
        out_re[k], out_im[k] = even_re[k] + tr, even_im[k] + ti
        out_re[k + half], out_im[k + half] = even_re[k] - tr, even_im[k] - ti
    return out_re, out_im


def kernel(
    sizes,
    codes_ref, table_ref,
    fields_ref, shots_ref, vel_ref, src_ref, whi_ref, wlo_ref, twist_ref,
    out_ref, image_ref,
    prop, lens, sends, recvs, enc, rec_out, rec_in, image_acc, image_send, image_in,
    send_sem, recv_sem, rec_send_sem, rec_sem, image_send_sem, image_sem,
):
    depth_n, lane_n, freqs, ticks, steps, shots_here, levels, points = sizes
    outer = points // LANES
    half_outer = outer // 2
    per_lane = steps // lane_n
    depth = lax.axis_index("depth")
    lane = lax.axis_index("lane")
    freq_total = freqs * lane_n
    rows = 2 * freqs

    barrier = pltpu.get_barrier_semaphore()

    def greet(d, l):
        pl.semaphore_signal(barrier, inc=1, device_id=(d, l), device_id_type=MESH)

    @pl.when(depth == 0)
    def _():
        for d in range(1, depth_n):
            greet(d, lane)

    @pl.when(depth > 0)
    def _():
        greet(0, lane)

    @pl.when(depth > 1)
    def _():
        greet(depth - 1, lane)

    @pl.when((depth > 0) & (depth < depth_n - 1))
    def _():
        greet(depth + 1, lane)

    for off in range(1, lane_n):
        greet(depth, lax.rem(lane + off, lane_n))

    row = lax.broadcasted_iota(jnp.int32, (rows, LANES), 0)
    freq_row = jnp.where(row >= freqs, row - freqs, row)
    for t in range(ticks):
        for j in range(shots_here):
            code = jnp.zeros((rows, LANES), jnp.int32)
            for f in range(freqs):
                value = codes_ref[t, depth * shots_here + j, f]
                code = jnp.where(freq_row == f, value, code)
            sin_e, cos_e = sincos(code.astype(F32) * (TWO_PI / CODES))
            enc[t, j, 0] = cos_e
            enc[t, j, 1] = sin_e

    def chunk(a):
        return slice(a * LANES, (a + 1) * LANES)

    for t in range(ticks):
        for a in range(half_outer):
            total_re, total_im = None, None
            for j in range(shots_here):
                pair = [
                    jnp.concatenate(
                        [shots_ref[t, j, c, :, chunk(a)], shots_ref[t, j, c, :, chunk(a + half_outer)]],
                        axis=0,
                    )
                    for c in range(2)
                ]
                c, s = enc[t, j, 0], enc[t, j, 1]
                re = c * pair[0] - s * pair[1]
                im = c * pair[1] + s * pair[0]
                total_re = re if total_re is None else total_re + re
                total_im = im if total_im is None else total_im + im
            rec_out[t, 0, a] = total_re
            rec_out[t, 1, a] = -total_im

    greeted = jnp.where(
        depth == 0,
        depth_n - 1,
        1 + (depth > 1).astype(jnp.int32) + (depth < depth_n - 1).astype(jnp.int32),
    ) + (lane_n - 1)
    pl.semaphore_wait(barrier, greeted)

    def rec_copy(t):
        return pltpu.make_async_remote_copy(
            src_ref=rec_out.at[t],
            dst_ref=rec_in.at[t, jnp.maximum(depth - 1, 0)],
            send_sem=rec_send_sem.at[t],
            recv_sem=rec_sem.at[t],
            device_id=(0, lane),
            device_id_type=MESH,
        )

    @pl.when(depth > 0)
    def _():
        for t in range(ticks):
            rec_copy(t).start()

    omega = OMEGA_LO + OMEGA_STEP * (lane * freqs + freq_row).astype(F32)
    index = vel_ref[...]
    slow_all = jnp.zeros((steps, points), F32)
    for l in range(levels):
        slow_all = jnp.where(index == l, table_ref[l], slow_all)
    ref_all = jnp.sum(slow_all, axis=1, keepdims=True) * (1.0 / points)
    column = lax.broadcasted_iota(jnp.int32, (rows, LANES), 1)
    for z in range(steps):
        ref_z = ref_all[z : z + 1, :]
        omega_ref = omega * ref_z
        for a in range(outer):
            m = a + outer * column
            m = jnp.where(m < points // 2, m, m - points)
            kx = m.astype(F32) * (TWO_PI / points)
            kz_sq = omega_ref * omega_ref - kx * kx
            phase = jnp.sqrt(jnp.maximum(kz_sq, 0.0)) * DEPTH_STEP
            damp = jnp.exp(-jnp.sqrt(jnp.maximum(-kz_sq, 0.0)) * DEPTH_STEP) * (1.0 / points)
            s, c = sincos(phase)
            prop[z, 0, a] = damp * c
            prop[z, 1, a] = damp * s
            angle = omega * (slow_all[z : z + 1, chunk(a)] - ref_z) * DEPTH_STEP
            s, c = sincos(angle)
            lens[z, 0, a] = c
            lens[z, 1, a] = s

    image_acc[...] = jnp.zeros_like(image_acc)

    def inner_dft(re, im):
        left = jnp.concatenate(re, axis=0)
        right = jnp.concatenate(im, axis=0)
        x = jnp.concatenate([left, right], axis=1)
        high = x.astype(BF16)
        low = (x - high.astype(F32)).astype(BF16)
        y = jnp.dot(high, whi_ref[...], preferred_element_type=F32)
        y = y + jnp.dot(low, whi_ref[...], preferred_element_type=F32)
        y = y + jnp.dot(high, wlo_ref[...], preferred_element_type=F32)
        y_re = [y[a * rows : (a + 1) * rows, :LANES] for a in range(outer)]
        y_im = [y[a * rows : (a + 1) * rows, LANES:] for a in range(outer)]
        return y_re, y_im

    def times(re, im, c, s):
        return re * c - im * s, re * s + im * c

    def step(k, state):
        re, im = list(state[:outer]), list(state[outer:])
        re, im = dft_across(re, im)
        for a in range(1, outer):
            c, s = twist_ref[0, a : a + 1, :], twist_ref[1, a : a + 1, :]
            re[a], im[a] = times(re[a], im[a], c, -s)
        re, im = inner_dft(re, im)
        for a in range(outer):
            re[a], im[a] = times(re[a], im[a], prop[k, 0, a], prop[k, 1, a])
        im, re = inner_dft(im, re)
        for a in range(1, outer):
            c, s = twist_ref[0, a : a + 1, :], twist_ref[1, a : a + 1, :]
            re[a], im[a] = times(re[a], im[a], c, s)
        im, re = dft_across(im, re)
        for a in range(outer):
            re[a], im[a] = times(re[a], im[a], lens[k, 0, a], lens[k, 1, a])
            image_acc[k, a] += re[a] * pltpu.roll(re[a], freqs, 0) - im[a] * pltpu.roll(
                im[a], freqs, 0
            )
        return tuple(re) + tuple(im)

    def field_copy(t):
        return pltpu.make_async_remote_copy(
            src_ref=sends.at[t],
            dst_ref=recvs.at[t],
            send_sem=send_sem.at[t],
            recv_sem=recv_sem.at[t],
            device_id=(jnp.minimum(depth + 1, depth_n - 1), lane),
            device_id_type=MESH,
        )

    def image_copy(k):
        return pltpu.make_async_remote_copy(
            src_ref=image_send.at[k],
            dst_ref=image_in.at[k % per_lane, lane],
            send_sem=image_send_sem.at[k],
            recv_sem=image_sem.at[k % per_lane, lane],
            device_id=(depth, k // per_lane),
            device_id_type=MESH,
        )

    for t in range(ticks):
        if t == 0:
            re = [
                jnp.concatenate([fields_ref[0, 0, :, chunk(a)], fields_ref[0, 2, :, chunk(a)]], axis=0)
                for a in range(outer)
            ]
            im = [
                jnp.concatenate([fields_ref[0, 1, :, chunk(a)], -fields_ref[0, 3, :, chunk(a)]], axis=0)
                for a in range(outer)
            ]
        else:
            re = [recvs[t - 1, 0, a] for a in range(outer)]
            im = [recvs[t - 1, 1, a] for a in range(outer)]
        state = lax.fori_loop(0, steps, step, tuple(re) + tuple(im))
        for a in range(outer):
            sends[t, 0, a] = state[a]
            sends[t, 1, a] = state[outer + a]

        @pl.when(depth < depth_n - 1)
        def _():
            field_copy(t).start()

        if t == ticks - 1:
            for k in range(steps):
                packed = jnp.zeros((outer, LANES), F32)
                place = lax.broadcasted_iota(jnp.int32, (outer, LANES), 0)
                for a in range(outer):
                    total = jnp.sum(image_acc[k, a][:freqs], axis=0, keepdims=True)
                    packed = jnp.where(place == a, total, packed)
                image_send[k] = packed * (1.0 / freq_total)

                @pl.when(lane != k // per_lane)
                def _():
                    image_copy(k).start()

        @pl.when(depth == 0)
        def _():
            pltpu.make_async_copy(rec_in.at[t], rec_in.at[t], rec_sem.at[t]).wait()
            for c in range(2):
                for a in range(half_outer):
                    total = rec_out[t, c, a]
                    for d in range(depth_n - 1):
                        total = total + rec_in[t, d, c, a]
                    for side in range(2):
                        where = a + side * half_outer
                        rec = total[side * freqs : (side + 1) * freqs]
                        recvs[t, c, where] = jnp.concatenate(
                            [src_ref[t, c, :, chunk(where)], rec], axis=0
                        )

        @pl.when(depth > 0)
        def _():
            pltpu.make_async_copy(recvs.at[t], recvs.at[t], recv_sem.at[t]).wait()

    for a in range(outer):
        re, im = recvs[ticks - 1, 0, a], recvs[ticks - 1, 1, a]
        out_ref[0, 0, :, chunk(a)] = re[:freqs]
        out_ref[0, 1, :, chunk(a)] = im[:freqs]
        out_ref[0, 2, :, chunk(a)] = re[freqs:]
        out_ref[0, 3, :, chunk(a)] = -im[freqs:]

    for i in range(per_lane):
        total = image_send[lane * per_lane + i]
        for l in range(lane_n):

            @pl.when(lane != l)
            def _():
                pltpu.make_async_copy(
                    image_in.at[i, l], image_in.at[i, l], image_sem.at[i, l]
                ).wait()

            total = total + jnp.where(lane != l, image_in[i, l], 0.0)
        for a in range(outer):
            image_ref[i : i + 1, chunk(a)] = total[a : a + 1, :]

    for t in range(ticks):

        @pl.when(depth < depth_n - 1)
        def _():
            field_copy(t).wait_send()

        @pl.when(depth > 0)
        def _():
            rec_copy(t).wait_send()

    for k in range(steps):

        @pl.when(lane != k // per_lane)
        def _():
            image_copy(k).wait_send()


def solution(mesh):
    depth_n, lane_n = mesh.shape["depth"], mesh.shape["lane"]

    def per_device(fields_in, shot_data, codes, vel_index, slowness_table):
        _, planes, freqs, points = fields_in.shape
        ticks, shots_here = shot_data.shape[0], shot_data.shape[1]
        shot_total = codes.shape[1]
        steps = vel_index.shape[0]
        levels = slowness_table.shape[0]
        outer = points // LANES
        rows = 2 * freqs
        per_lane = steps // lane_n
        angles = jnp.transpose(codes, (0, 2, 1)).astype(F32) * (TWO_PI / CODES)
        marker = (jnp.arange(points // shot_total) == 0).astype(F32)
        src = jnp.stack([jnp.cos(angles), jnp.sin(angles)], axis=1)
        src = (src[..., None] * marker).reshape(ticks, 2, freqs, points)
        high, low = dft_matrix(LANES)
        twist = twist_tables(outer, LANES)
        sizes = (depth_n, lane_n, freqs, ticks, steps, shots_here, levels, points)
        vmem = pl.BlockSpec(memory_space=pltpu.VMEM)
        smem = pl.BlockSpec(memory_space=pltpu.SMEM)
        return pl.pallas_call(
            functools.partial(kernel, sizes),
            out_shape=(
                jax.ShapeDtypeStruct(fields_in.shape, F32),
                jax.ShapeDtypeStruct((per_lane, points), F32),
            ),
            in_specs=[smem, smem] + [vmem] * 7,
            out_specs=(vmem, vmem),
            scratch_shapes=[
                pltpu.VMEM((steps, 2, outer, rows, LANES), F32),
                pltpu.VMEM((steps, 2, outer, rows, LANES), F32),
                pltpu.VMEM((ticks, 2, outer, rows, LANES), F32),
                pltpu.VMEM((ticks, 2, outer, rows, LANES), F32),
                pltpu.VMEM((ticks, shots_here, 2, rows, LANES), F32),
                pltpu.VMEM((ticks, 2, outer // 2, rows, LANES), F32),
                pltpu.VMEM((ticks, depth_n - 1, 2, outer // 2, rows, LANES), F32),
                pltpu.VMEM((steps, outer, rows, LANES), F32),
                pltpu.VMEM((steps, outer, LANES), F32),
                pltpu.VMEM((per_lane, lane_n, outer, LANES), F32),
                pltpu.SemaphoreType.DMA((ticks,)),
                pltpu.SemaphoreType.DMA((ticks,)),
                pltpu.SemaphoreType.DMA((ticks,)),
                pltpu.SemaphoreType.DMA((ticks,)),
                pltpu.SemaphoreType.DMA((steps,)),
                pltpu.SemaphoreType.DMA((per_lane, lane_n)),
            ],
            compiler_params=pltpu.CompilerParams(collective_id=0, has_side_effects=True),
            name="migrate",
        )(
            codes, slowness_table, fields_in, shot_data, vel_index, src,
            jnp.asarray(high), jnp.asarray(low), jnp.asarray(twist),
        )

    return jax.shard_map(
        per_device,
        mesh=mesh,
        in_specs=(
            P("depth", None, "lane", None),
            P(None, "depth", None, "lane", None),
            P(None, None, "lane"),
            P("depth", None),
            P(),
        ),
        out_specs=(P("depth", None, "lane", None), P(("depth", "lane"), None)),
        check_vma=False,
    )
```

profile of v0, /device:TPU:2, one launch (start us, length us, event | category | flops | bytes accessed | tf_op | source)
XLA Modules:
  0.0 29.1 jit_solution(1864280859563217027)
XLA Ops:
  0.6 0.8 %cosine_bitcast_fusion = (f32[4,1,4,16]{3,2,0,1:T(4,128)S(1)}, f32[4,1,4,16]{3,2,0,1:T(4,128)S(1)}) fusion(s32[4,16,4]{1,2,0:T(4,128)} %param.10), kind=kLoop, calls=%fused_computation.3 | loop fusion | flops 512 | bytes 3072 | tf_op jit(solution)/shard_map/stack | solution.py:372
  1.4 0.1 mul.29
  1.6 0.2 mul.30
  1.7 0.1 mul.32
  1.8 0.0 copy-start
  1.8 0.7 %broadcast_multiply_fusion.src_ref = f32[4,2,4,1024]{3,2,1,0:T(4,128)} fusion(f32[4,2,4,1024]{3,2,1,0:T(4,128)S(1)} %mul.30, f32[1024]{0:T(1024)S(1)} %mul.32), kind=kLoop, calls=%fused_computation | loop fusion | flops 32768 | bytes 266240 | tf_op jit(solution)/shard_map/mul | solution.py:373
  2.5 0.0 copy-done
  2.5 0.7 %copy.11.codes_ref = s32[4,16,4]{2,1,0:T(8,128)} copy(s32[4,16,4]{1,2,0:T(4,128)S(1)} %copy-done) | data formatting | bytes 2048 | tf_op args[2]
  3.2 23.8 %migrate.1 = (f32[1,4,4,1024]{3,2,1,0:T(4,128)}, f32[1,1024]{1,0:T(1,128)}) custom-call(s32[4,16,4]{2,1,0:T(8,128)} %copy.11.codes_ref, f32[64]{0:T(128)} %table_ref.1, f32[1,4,4,1024]{3,2,1,0:T(4,128)} %fields_ref.1, f32[4,2,2,4,1024]{4,3,2,1,0:T(4,128)} %shots_ref.1, s32[4,1024]{1,0:T(4,128)} %vel_ref.1, f32[4,2,4,1024]{3,2,1,0:T(4,128)} %broadcast_multiply_fusion.src_ref, ...), custom_call_target="tpu_custom_call" | custom-call | tf_op jit(solution)/shard_map/migrate/pallas_call | solution.py:379
  27.0 0.0 copy-start.1
  27.0 1.5 %copy.14 = f32[1,4,4,1024]{3,2,1,0:T(4,128)} copy(f32[1,4,4,1024]{3,2,1,0:T(4,128)} %get-tuple-element.6) | data formatting | bytes 131072
  28.5 0.0 copy-done.1
  28.5 0.6 %copy.15 = f32[1,1024]{1,0:T(1,128)} copy(f32[1,1024]{1,0:T(1,128)S(1)} %copy-done.1) | data formatting | bytes 8192
  (4 shorter events, 0.0 us)
Async XLA Ops:
  1.8 0.7 %copy-start = (s32[4,16,4]{1,2,0:T(4,128)S(1)}, s32[4,16,4]{1,2,0:T(4,128)}, u32[]{:S(2)}) copy-start(s32[4,16,4]{1,2,0:T(4,128)} %param.10) | copy-start | bytes 3076
  27.0 1.5 %copy-start.1 = (f32[1,1024]{1,0:T(1,128)S(1)}, f32[1,1024]{1,0:T(1,128)}, u32[]{:S(2)}) copy-start(f32[1,1024]{1,0:T(1,128)} %get-tuple-element.7) | copy-start | bytes 12292
where the time goes:
time: 29.4 us; the launch traced here: 29.1 us
  Pallas kernels  23.8 us (81%)
  local copies, waits for them, and re-layouts  3.16 us (11%)
  other arithmetic  1.46 us (5%)
  between operations  0.69 us (2%)
    pallas_call x1, Pallas kernels, per_device(): pl.pallas_call(functools.partial(kernel, sizes), out_shape=(jax.ShapeDtyp...  23.8 us
    unnamed x7, local copies, waits for them, and re-layouts  2.81 us
    another operation x2, other arithmetic, per_device(): src = jnp.stack([jnp.cos(angles), jnp.sin(angles)], axis=1)  0.78 us
    mul x1, other arithmetic, per_device(): src = (src[..., None] * marker).reshape(ticks, 2, freqs, points)  0.67 us

commit v1 on v0

--- a/solution.py
+++ b/solution.py
@@ -83,10 +83,11 @@
 
 def kernel(
     sizes,
-    codes_ref, table_ref,
-    fields_ref, shots_ref, vel_ref, src_ref, whi_ref, wlo_ref, twist_ref,
+    codes_hbm, table_hbm, shots_hbm, vel_hbm, fields_hbm, whi_hbm, wlo_hbm, twist_hbm,
     out_ref, image_ref,
-    prop, lens, sends, recvs, enc, rec_out, rec_in, image_acc, image_send, image_in,
+    codes_ref, code_rows, table_ref, shots_ref, vel_ref, fields_ref, whi_ref, wlo_ref, twist_ref,
+    load_sem,
+    prop, lens, sends, recvs, rec_out, rec_in, image_acc, image_send, image_in,
     send_sem, recv_sem, rec_send_sem, rec_sem, image_send_sem, image_sem,
 ):
     depth_n, lane_n, freqs, ticks, steps, shots_here, levels, points = sizes
@@ -98,6 +99,25 @@
     freq_total = freqs * lane_n
     rows = 2 * freqs
 
+    loads = [
+        pltpu.make_async_copy(src, dst, load_sem.at[i])
+        for i, (src, dst) in enumerate(
+            (
+                (codes_hbm, codes_ref),
+                (shots_hbm, shots_ref),
+                (table_hbm, table_ref),
+                (vel_hbm, vel_ref),
+                (fields_hbm, fields_ref),
+                (whi_hbm, whi_ref),
+                (wlo_hbm, wlo_ref),
+                (twist_hbm, twist_ref),
+                (codes_hbm, code_rows),
+            )
+        )
+    ]
+    for load in loads:
+        load.start()
+
     barrier = pltpu.get_barrier_semaphore()
 
     def greet(d, l):
@@ -125,20 +145,18 @@
 
     row = lax.broadcasted_iota(jnp.int32, (rows, LANES), 0)
     freq_row = jnp.where(row >= freqs, row - freqs, row)
-    for t in range(ticks):
+
+    def chunk(a):
+        return slice(a * LANES, (a + 1) * LANES)
+
+    def encode(t):
+        waves = []
         for j in range(shots_here):
             code = jnp.zeros((rows, LANES), jnp.int32)
             for f in range(freqs):
-                value = codes_ref[t, depth * shots_here + j, f]
+                value = codes_ref[t, f, depth * shots_here + j]
                 code = jnp.where(freq_row == f, value, code)
-            sin_e, cos_e = sincos(code.astype(F32) * (TWO_PI / CODES))
-            enc[t, j, 0] = cos_e
-            enc[t, j, 1] = sin_e
-
-    def chunk(a):
-        return slice(a * LANES, (a + 1) * LANES)
-
-    for t in range(ticks):
+            waves.append(sincos(code.astype(F32) * (TWO_PI / CODES)))
         for a in range(half_outer):
             total_re, total_im = None, None
             for j in range(shots_here):
@@ -149,20 +167,13 @@
                     )
                     for c in range(2)
                 ]
-                c, s = enc[t, j, 0], enc[t, j, 1]
+                s, c = waves[j]
                 re = c * pair[0] - s * pair[1]
                 im = c * pair[1] + s * pair[0]
                 total_re = re if total_re is None else total_re + re
                 total_im = im if total_im is None else total_im + im
             rec_out[t, 0, a] = total_re
             rec_out[t, 1, a] = -total_im
-
-    greeted = jnp.where(
-        depth == 0,
-        depth_n - 1,
-        1 + (depth > 1).astype(jnp.int32) + (depth < depth_n - 1).astype(jnp.int32),
-    ) + (lane_n - 1)
-    pl.semaphore_wait(barrier, greeted)
 
     def rec_copy(t):
         return pltpu.make_async_remote_copy(
@@ -174,10 +185,24 @@
             device_id_type=MESH,
         )
 
+    loads[0].wait()
+    loads[1].wait()
+    encode(0)
+    greeted = jnp.where(
+        depth == 0,
+        depth_n - 1,
+        1 + (depth > 1).astype(jnp.int32) + (depth < depth_n - 1).astype(jnp.int32),
+    ) + (lane_n - 1)
+    pl.semaphore_wait(barrier, greeted)
+
     @pl.when(depth > 0)
     def _():
-        for t in range(ticks):
-            rec_copy(t).start()
+        rec_copy(0).start()
+
+    for t in range(1, ticks):
+        encode(t)
+    for load in loads[2:]:
+        load.wait()
 
     omega = OMEGA_LO + OMEGA_STEP * (lane * freqs + freq_row).astype(F32)
     index = vel_ref[...]
@@ -212,8 +237,10 @@
         x = jnp.concatenate([left, right], axis=1)
         high = x.astype(BF16)
         low = (x - high.astype(F32)).astype(BF16)
-        y = jnp.dot(high, whi_ref[...], preferred_element_type=F32)
-        y = y + jnp.dot(low, whi_ref[...], preferred_element_type=F32)
+        both = jnp.dot(
+            jnp.concatenate([high, low], axis=0), whi_ref[...], preferred_element_type=F32
+        )
+        y = both[: outer * rows] + both[outer * rows :]
         y = y + jnp.dot(high, wlo_ref[...], preferred_element_type=F32)
         y_re = [y[a * rows : (a + 1) * rows, :LANES] for a in range(outer)]
         y_im = [y[a * rows : (a + 1) * rows, LANES:] for a in range(outer)]
@@ -263,6 +290,21 @@
             device_id_type=MESH,
         )
 
+    def sources():
+        shot_total = code_rows.shape[2]
+        spacing = points // shot_total
+        lane_index = lax.broadcasted_iota(jnp.int32, (freqs, LANES), 1)
+        for t in range(ticks):
+            sin_e, cos_e = sincos(code_rows[t].astype(F32) * (TWO_PI / CODES))
+            for c, wave in enumerate((cos_e, sin_e)):
+                for a in range(outer):
+                    value = jnp.zeros((freqs, LANES), F32)
+                    for j in range(shot_total):
+                        place = j * spacing - a * LANES
+                        if 0 <= place < LANES:
+                            value = jnp.where(lane_index == place, wave[:, j : j + 1], value)
+                    recvs[t, c, a, :freqs] = value
+
     for t in range(ticks):
         if t == 0:
             re = [
@@ -285,6 +327,12 @@
         def _():
             field_copy(t).start()
 
+        if t + 1 < ticks:
+
+            @pl.when(depth > 0)
+            def _():
+                rec_copy(t + 1).start()
+
         if t == ticks - 1:
             for k in range(steps):
                 packed = jnp.zeros((outer, LANES), F32)
@@ -300,6 +348,8 @@
 
         @pl.when(depth == 0)
         def _():
+            if t == 0:
+                sources()
             pltpu.make_async_copy(rec_in.at[t], rec_in.at[t], rec_sem.at[t]).wait()
             for c in range(2):
                 for a in range(half_outer):
@@ -309,9 +359,7 @@
                     for side in range(2):
                         where = a + side * half_outer
                         rec = total[side * freqs : (side + 1) * freqs]
-                        recvs[t, c, where] = jnp.concatenate(
-                            [src_ref[t, c, :, chunk(where)], rec], axis=0
-                        )
+                        recvs[t, c, where, freqs:] = rec
 
         @pl.when(depth > 0)
         def _():
@@ -367,29 +415,35 @@
         outer = points // LANES
         rows = 2 * freqs
         per_lane = steps // lane_n
-        angles = jnp.transpose(codes, (0, 2, 1)).astype(F32) * (TWO_PI / CODES)
-        marker = (jnp.arange(points // shot_total) == 0).astype(F32)
-        src = jnp.stack([jnp.cos(angles), jnp.sin(angles)], axis=1)
-        src = (src[..., None] * marker).reshape(ticks, 2, freqs, points)
+        codes = jnp.transpose(codes, (0, 2, 1))
         high, low = dft_matrix(LANES)
         twist = twist_tables(outer, LANES)
         sizes = (depth_n, lane_n, freqs, ticks, steps, shots_here, levels, points)
+        anywhere = pl.BlockSpec(memory_space=pl.ANY)
         vmem = pl.BlockSpec(memory_space=pltpu.VMEM)
-        smem = pl.BlockSpec(memory_space=pltpu.SMEM)
-        return pl.pallas_call(
+        fields_out, image = pl.pallas_call(
             functools.partial(kernel, sizes),
             out_shape=(
-                jax.ShapeDtypeStruct(fields_in.shape, F32),
-                jax.ShapeDtypeStruct((per_lane, points), F32),
+                pltpu.VMEM(fields_in.shape, F32),
+                pltpu.VMEM((per_lane, points), F32),
             ),
-            in_specs=[smem, smem] + [vmem] * 7,
+            in_specs=[anywhere] * 8,
             out_specs=(vmem, vmem),
             scratch_shapes=[
+                pltpu.SMEM(codes.shape, jnp.int32),
+                pltpu.VMEM(codes.shape, jnp.int32),
+                pltpu.SMEM(slowness_table.shape, F32),
+                pltpu.VMEM(shot_data.shape, F32),
+                pltpu.VMEM(vel_index.shape, jnp.int32),
+                pltpu.VMEM(fields_in.shape, F32),
+                pltpu.VMEM(high.shape, BF16),
+                pltpu.VMEM(low.shape, BF16),
+                pltpu.VMEM(twist.shape, F32),
+                pltpu.SemaphoreType.DMA((9,)),
                 pltpu.VMEM((steps, 2, outer, rows, LANES), F32),
                 pltpu.VMEM((steps, 2, outer, rows, LANES), F32),
                 pltpu.VMEM((ticks, 2, outer, rows, LANES), F32),
                 pltpu.VMEM((ticks, 2, outer, rows, LANES), F32),
-                pltpu.VMEM((ticks, shots_here, 2, rows, LANES), F32),
                 pltpu.VMEM((ticks, 2, outer // 2, rows, LANES), F32),
                 pltpu.VMEM((ticks, depth_n - 1, 2, outer // 2, rows, LANES), F32),
                 pltpu.VMEM((steps, outer, rows, LANES), F32),
@@ -405,9 +459,10 @@
             compiler_params=pltpu.CompilerParams(collective_id=0, has_side_effects=True),
             name="migrate",
         )(
-            codes, slowness_table, fields_in, shot_data, vel_index, src,
+            codes, slowness_table, shot_data, vel_index, fields_in,
             jnp.asarray(high), jnp.asarray(low), jnp.asarray(twist),
         )
+        return fields_out, image
 
     return jax.shard_map(
         per_device,

time: 29.4 us -> 22.8 us (0.78)
  the two profiles are of different devices: /device:TPU:2 before, /device:TPU:0 now
where the time goes in v1:
time: 22.8 us; the launch traced here: 22.6 us
  Pallas kernels  20.8 us (91%)
  local copies, waits for them, and re-layouts  1.22 us (5%)
  between operations  0.64 us (3%)
    pallas_call x1, Pallas kernels, per_device(): pl.pallas_call(functools.partial(kernel, sizes), out_shape=(pltpu.VMEM(fi...  20.8 us
    unnamed x2, local copies, waits for them, and re-layouts  1.22 us

profile of v1, /device:TPU:0, one launch (start us, length us, event | category | flops | bytes accessed | tf_op | source)
XLA Modules:
  0.0 22.6 jit_solution(2648469298632207719)
XLA Ops:
  0.6 20.8 %migrate.1 = (f32[1,4,4,1024]{3,2,1,0:T(4,128)S(1)}, f32[1,1024]{1,0:T(1,128)S(1)}) custom-call(s32[4,4,16]{2,1,0:T(4,128)} %bitcast.1, f32[64]{0:T(128)} %table_hbm.1, f32[4,2,2,4,1024]{4,3,2,1,0:T(4,128)} %shots_hbm.1, s32[4,1024]{1,0:T(4,128)} %vel_hbm.1, f32[1,4,4,1024]{3,2,1,0:T(4,128)} %fields_hbm.1, bf16[256,256]{1,0:T(8,128)(2,1)} %constant.6.clone.whi_hbm, ...), custom_call_target="tpu_custom_call" | custom-call | tf_op jit(solution)/shard_map/migrate/pallas_call | solution.py:424
  21.4 0.6 %copy.12 = f32[1,4,4,1024]{3,2,1,0:T(4,128)} copy(f32[1,4,4,1024]{3,2,1,0:T(4,128)S(1)} %get-tuple-element.2) | data formatting | bytes 131072
  22.0 0.6 %copy.13 = f32[1,1024]{1,0:T(1,128)} copy(f32[1,1024]{1,0:T(1,128)S(1)} %get-tuple-element.3) | data formatting | bytes 8192

commit v2 on v1

--- a/solution.py
+++ b/solution.py
@@ -188,17 +188,6 @@
     loads[0].wait()
     loads[1].wait()
     encode(0)
-    greeted = jnp.where(
-        depth == 0,
-        depth_n - 1,
-        1 + (depth > 1).astype(jnp.int32) + (depth < depth_n - 1).astype(jnp.int32),
-    ) + (lane_n - 1)
-    pl.semaphore_wait(barrier, greeted)
-
-    @pl.when(depth > 0)
-    def _():
-        rec_copy(0).start()
-
     for t in range(1, ticks):
         encode(t)
     for load in loads[2:]:
@@ -322,6 +311,18 @@
         for a in range(outer):
             sends[t, 0, a] = state[a]
             sends[t, 1, a] = state[outer + a]
+
+        if t == 0:
+            greeted = jnp.where(
+                depth == 0,
+                depth_n - 1,
+                1 + (depth > 1).astype(jnp.int32) + (depth < depth_n - 1).astype(jnp.int32),
+            ) + (lane_n - 1)
+            pl.semaphore_wait(barrier, greeted)
+
+            @pl.when(depth > 0)
+            def _():
+                rec_copy(0).start()
 
         @pl.when(depth < depth_n - 1)
         def _():

time: 22.8 us -> 23.6 us (1.035)
  the two profiles are of different devices: /device:TPU:0 before, /device:TPU:2 now
where the time goes in v2:
time: 23.6 us; the launch traced here: 23.4 us
  Pallas kernels  21.6 us (92%)
  local copies, waits for them, and re-layouts  1.22 us (5%)
  between operations  0.64 us (3%)
    pallas_call x1, Pallas kernels, per_device(): pl.pallas_call(functools.partial(kernel, sizes), out_shape=(pltpu.VMEM(fi...  21.6 us
    unnamed x2, local copies, waits for them, and re-layouts  1.22 us

profile of v2, /device:TPU:2, one launch (start us, length us, event | category | flops | bytes accessed | tf_op | source)
XLA Modules:
  0.0 23.4 jit_solution(5188371326841043783)
XLA Ops:
  0.6 21.6 %migrate.1 = (f32[1,4,4,1024]{3,2,1,0:T(4,128)S(1)}, f32[1,1024]{1,0:T(1,128)S(1)}) custom-call(s32[4,4,16]{2,1,0:T(4,128)} %bitcast.1, f32[64]{0:T(128)} %table_hbm.1, f32[4,2,2,4,1024]{4,3,2,1,0:T(4,128)} %shots_hbm.1, s32[4,1024]{1,0:T(4,128)} %vel_hbm.1, f32[1,4,4,1024]{3,2,1,0:T(4,128)} %fields_hbm.1, bf16[256,256]{1,0:T(8,128)(2,1)} %constant.6.clone.whi_hbm, ...), custom_call_target="tpu_custom_call" | custom-call | tf_op jit(solution)/shard_map/migrate/pallas_call | solution.py:425
  22.2 0.6 %copy.12 = f32[1,4,4,1024]{3,2,1,0:T(4,128)} copy(f32[1,4,4,1024]{3,2,1,0:T(4,128)S(1)} %get-tuple-element.2) | data formatting | bytes 131072
  22.8 0.6 %copy.13 = f32[1,1024]{1,0:T(1,128)} copy(f32[1,1024]{1,0:T(1,128)S(1)} %get-tuple-element.3) | data formatting | bytes 8192

commit v3 on v1

--- a/solution.py
+++ b/solution.py
@@ -199,8 +199,6 @@
     def _():
         rec_copy(0).start()
 
-    for t in range(1, ticks):
-        encode(t)
     for load in loads[2:]:
         load.wait()
 
@@ -328,10 +326,7 @@
             field_copy(t).start()
 
         if t + 1 < ticks:
-
-            @pl.when(depth > 0)
-            def _():
-                rec_copy(t + 1).start()
+            encode(t + 1)
 
         if t == ticks - 1:
             for k in range(steps):
@@ -364,6 +359,8 @@
         @pl.when(depth > 0)
         def _():
             pltpu.make_async_copy(recvs.at[t], recvs.at[t], recv_sem.at[t]).wait()
+            if t + 1 < ticks:
+                rec_copy(t + 1).start()
 
     for a in range(outer):
         re, im = recvs[ticks - 1, 0, a], recvs[ticks - 1, 1, a]

time: 22.8 us -> 24 us (1.053)
  Pallas kernels: 20.8 us -> 21.9 us
    pallas_call x1, Pallas kernels: 20.8 us -> 21.9 us  [per_device(): pl.pallas_call(functools.partial(kernel, sizes), out_shape=(pltpu.VMEM(fi...]
where the time goes in v3:
time: 24 us; the launch traced here: 23.8 us
  Pallas kernels  21.9 us (91%)
  local copies, waits for them, and re-layouts  1.22 us (5%)
  between operations  0.64 us (3%)
    pallas_call x1, Pallas kernels, per_device(): pl.pallas_call(functools.partial(kernel, sizes), out_shape=(pltpu.VMEM(fi...  21.9 us
    unnamed x2, local copies, waits for them, and re-layouts  1.22 us

profile of v3, /device:TPU:0, one launch (start us, length us, event | category | flops | bytes accessed | tf_op | source)
XLA Modules:
  0.0 23.8 jit_solution(16598034865598862481)
XLA Ops:
  0.6 21.9 %migrate.1 = (f32[1,4,4,1024]{3,2,1,0:T(4,128)S(1)}, f32[1,1024]{1,0:T(1,128)S(1)}) custom-call(s32[4,4,16]{2,1,0:T(4,128)} %bitcast.1, f32[64]{0:T(128)} %table_hbm.1, f32[4,2,2,4,1024]{4,3,2,1,0:T(4,128)} %shots_hbm.1, s32[4,1024]{1,0:T(4,128)} %vel_hbm.1, f32[1,4,4,1024]{3,2,1,0:T(4,128)} %fields_hbm.1, bf16[256,256]{1,0:T(8,128)(2,1)} %constant.6.clone.whi_hbm, ...), custom_call_target="tpu_custom_call" | custom-call | tf_op jit(solution)/shard_map/migrate/pallas_call | solution.py:421
  22.6 0.6 %copy.12 = f32[1,4,4,1024]{3,2,1,0:T(4,128)} copy(f32[1,4,4,1024]{3,2,1,0:T(4,128)S(1)} %get-tuple-element.2) | data formatting | bytes 131072
  23.2 0.6 %copy.13 = f32[1,1024]{1,0:T(1,128)} copy(f32[1,1024]{1,0:T(1,128)S(1)} %get-tuple-element.3) | data formatting | bytes 8192
